TPU v7x, 32 devices: a whole 2x2x4 slice. The times are simulated.
32 devices in a mesh: dp: 2 (over x), gx: 4 (over y, core), gy: 4 (over z).
Axes of the slice: x: 2, y: 2, z: 4, core: 2. Of those that a mesh axis runs over, the one named last changes fastest.
Arguments:
- block_input: bfloat16 [64, 529, 768], P(('dp', 'gx', 'gy')), may hold values from -6 to 6
- segment_ids: int32 [64, 529], P(('dp', 'gx', 'gy')), may hold values from 0 to 5, never falling along the last dimension, each value on 1 to 264 neighbouring positions
- out_grad: bfloat16 [64, 529, 768], P(('dp', 'gx', 'gy')), may hold values from -6 to 6
- query_weight: bfloat16 [768, 768], P(('dp', 'gx', 'gy')), may hold values from -0.21875 to 0.21875
- key_weight: bfloat16 [768, 768], P(('dp', 'gx', 'gy')), may hold values from -0.21875 to 0.21875
- value_weight: bfloat16 [768, 768], P(('dp', 'gx', 'gy')), may hold values from -0.21875 to 0.21875
- output_weight: bfloat16 [768, 768], P(('dp', 'gx', 'gy')), may hold values from -0.875 to 0.875
- first_gain: bfloat16 [768], P(('dp', 'gx', 'gy')), may hold values from 0.25 to 1.75
- first_shift: bfloat16 [768], P(('dp', 'gx', 'gy')), may hold values from -3 to 3
- query_bias: bfloat16 [768], P(('dp', 'gx', 'gy')), may hold values from -3 to 3
- value_bias: bfloat16 [768], P(('dp', 'gx', 'gy')), may hold values from -3 to 3
- output_bias: bfloat16 [768], P(('dp', 'gx', 'gy')), may hold values from -3 to 3
- second_gain: bfloat16 [768], P(('dp', 'gx', 'gy')), may hold values from 0.25 to 1.75
- second_shift: bfloat16 [768], P(('dp', 'gx', 'gy')), may hold values from -3 to 3
- up_weight: bfloat16 [768, 3072], P(('dp', 'gy'), 'gx'), may hold values from -0.21875 to 0.21875
- up_bias: bfloat16 [3072], P(('dp', 'gx', 'gy')), may hold values from -3 to 3
- down_weight: bfloat16 [768, 3072], P(('dp', 'gy'), 'gx'), may hold values from -0.15625 to 0.15625
- down_bias: bfloat16 [768], P(('dp', 'gx', 'gy')), may hold values from -3 to 3
Outputs:
- block_output: bfloat16 [64, 529, 768], P(('dp', 'gx', 'gy'))
- input_grad: bfloat16 [64, 529, 768], P(('dp', 'gx', 'gy'))
- query_weight_grad: float32 [768, 768], P(('dp', 'gx', 'gy'))
- key_weight_grad: float32 [768, 768], P(('dp', 'gx', 'gy'))
- value_weight_grad: float32 [768, 768], P(('dp', 'gx', 'gy'))
- output_weight_grad: float32 [768, 768], P(('dp', 'gx', 'gy'))
- first_gain_grad: float32 [768], P(('dp', 'gx', 'gy'))
- first_shift_grad: float32 [768], P(('dp', 'gx', 'gy'))
- query_bias_grad: float32 [768], P(('dp', 'gx', 'gy'))
- value_bias_grad: float32 [768], P(('dp', 'gx', 'gy'))
- output_bias_grad: float32 [768], P(('dp', 'gx', 'gy'))
- second_gain_grad: float32 [768], P(('dp', 'gx', 'gy'))
- second_shift_grad: float32 [768], P(('dp', 'gx', 'gy'))
- up_weight_grad: float32 [768, 3072], P(('dp', 'gy'), 'gx')
- up_bias_grad: float32 [3072], P(('dp', 'gx', 'gy'))
- down_weight_grad: float32 [768, 3072], P(('dp', 'gy'), 'gx')
- down_bias_grad: float32 [768], P(('dp', 'gx', 'gy'))
Inputs may be any that keep to these rules, and one draw needn't show every extreme that they name: `segment_ids`: in each strip the document numbers never fall and every one of the 6 documents takes one or more slots; none takes more than half of 529 (rounded down) slots, and one takes exactly that many.
All inputs are finite; a program needn't handle non-finite values.
Results may differ from a plain program's by a relative error of at most 0.017.
Values may be sent and summed in bfloat16 or wider, within the bound.
A program may use at most 192 MiB of HBM per device.

v0:
```python
import jax
import jax.numpy as jnp
from jax import lax
from jax.sharding import PartitionSpec as P

H = 12
HD = 64


def norm_rows(in_rows, norm_gain, norm_shift):
    centred = in_rows - jnp.mean(in_rows, axis=-1, keepdims=True)
    variance = jnp.mean(centred * centred, axis=-1, keepdims=True)
    return centred * lax.rsqrt(variance + 1e-06) * norm_gain + norm_shift


def exact_gelu(pre_act):
    return jax.nn.gelu(pre_act, approximate=False)


def project(input_reduced, complete_weight):
    return jnp.einsum(
        "nxt,tp->nxp", input_reduced, complete_weight, preferred_element_type=jnp.float32
    )


def project_back(gradient_reduced, complete_weight):
    return jnp.einsum(
        "tkx,mx->tkm", gradient_reduced, complete_weight, preferred_element_type=jnp.float32
    )


def weight_grad(input_reduced, gradient_reduced):
    return jnp.einsum(
        "zvy,zvn->yn", input_reduced, gradient_reduced, preferred_element_type=jnp.float32
    )


def masked_scores(query_heads, key_heads, seg_row):
    same_doc = seg_row[:, None] == seg_row[None, :]
    raw_scores = (
        jnp.einsum("qhd,khd->hqk", query_heads, key_heads, preferred_element_type=jnp.float32)
        * 0.125
    )
    return jnp.where(same_doc[None], raw_scores, -1e30)


def attend_strip(operands):
    query_heads, key_heads, value_heads, seg_row = operands
    scores = masked_scores(query_heads, key_heads, seg_row)
    row_max = jnp.max(scores, axis=-1, keepdims=True)
    exp_rows = jnp.exp(scores - row_max)
    totals = jnp.sum(exp_rows, axis=-1, keepdims=True)
    prob_low = (exp_rows / totals).astype(jnp.bfloat16)
    head_mix = jnp.einsum("hqk,khd->qhd", prob_low, value_heads, preferred_element_type=jnp.float32)
    return (head_mix, row_max + jnp.log(totals))


def strip_backward(operands):
    query_heads, key_heads, value_heads, seg_row, log_total, mix_grad = operands
    scores = masked_scores(query_heads, key_heads, seg_row)
    prob_rows = jnp.exp(scores - log_total)
    value_grad = jnp.einsum(
        "hqk,qhd->khd", prob_rows.astype(jnp.bfloat16), mix_grad, preferred_element_type=jnp.float32
    )
    prob_grad = jnp.einsum(
        "qhd,khd->hqk", mix_grad, value_heads, preferred_element_type=jnp.float32
    )
    score_grad = prob_rows * (prob_grad - jnp.sum(prob_grad * prob_rows, axis=-1, keepdims=True))
    score_low = score_grad.astype(jnp.bfloat16)
    query_grad = (
        jnp.einsum("hqk,khd->qhd", score_low, key_heads, preferred_element_type=jnp.float32) * 0.125
    )
    key_grad = (
        jnp.einsum("hqk,qhd->khd", score_low, query_heads, preferred_element_type=jnp.float32)
        * 0.125
    )
    return (
        query_grad.astype(jnp.bfloat16),
        key_grad.astype(jnp.bfloat16),
        value_grad.astype(jnp.bfloat16),
    )


def fetch_params(
    query_weight,
    key_weight,
    value_weight,
    output_weight,
    first_gain,
    first_shift,
    query_bias,
    value_bias,
    output_bias,
    second_gain,
    second_shift,
    up_bias,
    down_bias,
):
    return (
        lax.all_gather(query_weight, ("dp", "gx", "gy"), axis=0, tiled=True),
        lax.all_gather(key_weight, ("dp", "gx", "gy"), axis=0, tiled=True),
        lax.all_gather(value_weight, ("dp", "gx", "gy"), axis=0, tiled=True),
        lax.all_gather(output_weight, ("dp", "gx", "gy"), axis=0, tiled=True),
        lax.all_gather(first_gain, ("dp", "gx", "gy"), axis=0, tiled=True),
        lax.all_gather(first_shift, ("dp", "gx", "gy"), axis=0, tiled=True),
        lax.all_gather(query_bias, ("dp", "gx", "gy"), axis=0, tiled=True),
        lax.all_gather(value_bias, ("dp", "gx", "gy"), axis=0, tiled=True),
        lax.all_gather(output_bias, ("dp", "gx", "gy"), axis=0, tiled=True),
        lax.all_gather(second_gain, ("dp", "gx", "gy"), axis=0, tiled=True),
        lax.all_gather(second_shift, ("dp", "gx", "gy"), axis=0, tiled=True),
        lax.all_gather(up_bias, ("dp", "gx", "gy"), axis=0, tiled=True),
        lax.all_gather(down_bias, ("dp", "gx", "gy"), axis=0, tiled=True),
    )


def fetch_mlp(up_weight, down_weight):
    up_rows, down_projected_rows = (
        lax.all_gather(up_weight, ("dp", "gy"), axis=0, tiled=True),
        lax.all_gather(down_weight, ("dp", "gy"), axis=0, tiled=True),
    )
    return (up_rows, down_projected_rows)


def per_device(
    block_input,
    segment_ids,
    out_grad,
    query_weight,
    key_weight,
    value_weight,
    output_weight,
    first_gain,
    first_shift,
    query_bias,
    value_bias,
    output_bias,
    second_gain,
    second_shift,
    up_weight,
    up_bias,
    down_weight,
    down_bias,
):
    strips, length, model_width = block_input.shape
    head_shape = (strips, length, H, HD)
    (
        query_full,
        key_full,
        value_full,
        output_full,
        gain_one,
        shift_one,
        query_shift,
        value_shift,
        output_shift,
        gain_two,
        shift_two,
        up_shift,
        down_shift,
    ) = fetch_params(
        query_weight,
        key_weight,
        value_weight,
        output_weight,
        first_gain,
        first_shift,
        query_bias,
        value_bias,
        output_bias,
        second_gain,
        second_shift,
        up_bias,
        down_bias,
    )
    up_rows, down_projected_rows = fetch_mlp(up_weight, down_weight)
    gain_one = gain_one.astype(jnp.float32)
    shift_one = shift_one.astype(jnp.float32)
    gain_two = gain_two.astype(jnp.float32)
    shift_two = shift_two.astype(jnp.float32)
    inputs = block_input.astype(jnp.float32)
    normed, first_back = jax.vjp(norm_rows, inputs, gain_one, shift_one)
    normed_low = normed.astype(jnp.bfloat16)
    query_low = (project(normed_low, query_full) + query_shift.astype(jnp.float32)).astype(
        jnp.bfloat16
    )
    key_low = project(normed_low, key_full).astype(jnp.bfloat16)
    value_low = (project(normed_low, value_full) + value_shift.astype(jnp.float32)).astype(
        jnp.bfloat16
    )
    query_heads = query_low.reshape(head_shape)
    key_heads = key_low.reshape(head_shape)
    value_heads = value_low.reshape(head_shape)
    head_mix, log_total = lax.map(attend_strip, (query_heads, key_heads, value_heads, segment_ids))
    mixed_low = head_mix.reshape(strips, length, model_width).astype(jnp.bfloat16)
    residual = inputs + (project(mixed_low, output_full) + output_shift.astype(jnp.float32))
    second, second_back = jax.vjp(norm_rows, residual, gain_two, shift_two)
    second_low = second.astype(jnp.bfloat16)
    block_units = up_rows.shape[1]
    unit_start = lax.axis_index("gx") * block_units
    ff_rows = lax.all_gather(second_low, "gx", axis=0, tiled=True)
    up_local = lax.dynamic_slice_in_dim(up_shift.astype(jnp.float32), unit_start, block_units)
    hidden_pre = project(ff_rows, up_rows) + up_local
    hidden_act, gelu_back = jax.vjp(exact_gelu, hidden_pre)
    hidden_reduced = hidden_act.astype(jnp.bfloat16)
    down_slice_piece = jnp.einsum(
        "tkx,mx->tkm", hidden_reduced, down_projected_rows, preferred_element_type=jnp.float32
    )
    down_sum = lax.psum_scatter(
        down_slice_piece.astype(jnp.bfloat16), "gx", scatter_dimension=0, tiled=True
    ).astype(jnp.float32)
    result = residual + (down_sum + down_shift.astype(jnp.float32))
    fetched = fetch_params(
        query_weight,
        key_weight,
        value_weight,
        output_weight,
        first_gain,
        first_shift,
        query_bias,
        value_bias,
        output_bias,
        second_gain,
        second_shift,
        up_bias,
        down_bias,
    )
    query_full, key_full, value_full, output_full = (fetched[0], fetched[1], fetched[2], fetched[3])
    up_rows, down_projected_rows = fetch_mlp(up_weight, down_weight)
    gradient_row_block = lax.all_gather(out_grad, "gx", axis=0, tiled=True)
    hidden_grad = jnp.einsum(
        "nxt,tp->nxp", gradient_row_block, down_projected_rows, preferred_element_type=jnp.float32
    )
    pre_grad = gelu_back(hidden_grad)[0].astype(jnp.bfloat16)
    down_weight_grad = weight_grad(gradient_row_block, hidden_reduced)
    up_weight_grad = weight_grad(ff_rows, pre_grad)
    up_bias_part = jnp.sum(pre_grad, axis=(0, 1), dtype=jnp.float32)
    second_part = project_back(pre_grad, up_rows)
    second_grad = lax.psum_scatter(
        second_part.astype(jnp.bfloat16), "gx", scatter_dimension=0, tiled=True
    ).astype(jnp.float32)
    up_bias_grad = lax.dynamic_update_slice_in_dim(
        jnp.zeros((up_shift.shape[0],), jnp.float32), up_bias_part, unit_start, 0
    )
    up_weight_grad, down_weight_grad = (
        lax.psum_scatter(up_weight_grad, ("dp", "gy"), scatter_dimension=0, tiled=True),
        lax.psum_scatter(down_weight_grad, ("dp", "gy"), scatter_dimension=0, tiled=True),
    )
    down_bias_grad = jnp.sum(out_grad, axis=(0, 1), dtype=jnp.float32)
    norm_grad_res, gain_two_grad, shift_two_grad = second_back(second_grad)
    residual_grad = out_grad.astype(jnp.float32) + norm_grad_res
    branch_low = residual_grad.astype(jnp.bfloat16)
    output_bias_grad = jnp.sum(branch_low, axis=(0, 1), dtype=jnp.float32)
    output_weight_grad = weight_grad(mixed_low, branch_low)
    mixed_grad = project_back(branch_low, output_full).astype(jnp.bfloat16)
    query_grad, key_grad, value_grad = lax.map(
        strip_backward,
        (
            query_heads,
            key_heads,
            value_heads,
            segment_ids,
            log_total,
            mixed_grad.reshape(head_shape),
        ),
    )
    query_grad = query_grad.reshape(strips, length, model_width)
    key_grad = key_grad.reshape(strips, length, model_width)
    value_grad = value_grad.reshape(strips, length, model_width)
    query_weight_grad = weight_grad(normed_low, query_grad)
    key_weight_grad = weight_grad(normed_low, key_grad)
    value_weight_grad = weight_grad(normed_low, value_grad)
    query_bias_grad = jnp.sum(query_grad, axis=(0, 1), dtype=jnp.float32)
    value_bias_grad = jnp.sum(value_grad, axis=(0, 1), dtype=jnp.float32)
    normed_grad = (
        project_back(query_grad, query_full)
        + project_back(key_grad, key_full)
        + project_back(value_grad, value_full)
    )
    norm_grad_in, gain_one_grad, shift_one_grad = first_back(normed_grad)
    input_grad = (residual_grad + norm_grad_in).astype(jnp.bfloat16)
    summed = (
        lax.psum_scatter(query_weight_grad, ("dp", "gx", "gy"), scatter_dimension=0, tiled=True),
        lax.psum_scatter(key_weight_grad, ("dp", "gx", "gy"), scatter_dimension=0, tiled=True),
        lax.psum_scatter(value_weight_grad, ("dp", "gx", "gy"), scatter_dimension=0, tiled=True),
        lax.psum_scatter(output_weight_grad, ("dp", "gx", "gy"), scatter_dimension=0, tiled=True),
        lax.psum_scatter(gain_one_grad, ("dp", "gx", "gy"), scatter_dimension=0, tiled=True),
        lax.psum_scatter(shift_one_grad, ("dp", "gx", "gy"), scatter_dimension=0, tiled=True),
        lax.psum_scatter(query_bias_grad, ("dp", "gx", "gy"), scatter_dimension=0, tiled=True),
        lax.psum_scatter(value_bias_grad, ("dp", "gx", "gy"), scatter_dimension=0, tiled=True),
        lax.psum_scatter(output_bias_grad, ("dp", "gx", "gy"), scatter_dimension=0, tiled=True),
        lax.psum_scatter(gain_two_grad, ("dp", "gx", "gy"), scatter_dimension=0, tiled=True),
        lax.psum_scatter(shift_two_grad, ("dp", "gx", "gy"), scatter_dimension=0, tiled=True),
        lax.psum_scatter(up_bias_grad, ("dp", "gx", "gy"), scatter_dimension=0, tiled=True),
        lax.psum_scatter(down_bias_grad, ("dp", "gx", "gy"), scatter_dimension=0, tiled=True),
    )
    return (
        result.astype(jnp.bfloat16),
        input_grad,
        summed[0],
        summed[1],
        summed[2],
        summed[3],
        summed[4],
        summed[5],
        summed[6],
        summed[7],
        summed[8],
        summed[9],
        summed[10],
        up_weight_grad,
        summed[11],
        down_weight_grad,
        summed[12],
    )


def solution(mesh):
    placed = (
        P(("dp", "gx", "gy"), None, None),
        P(("dp", "gx", "gy"), None),
        P(("dp", "gx", "gy"), None, None),
        P(("dp", "gx", "gy"), None),
        P(("dp", "gx", "gy"), None),
        P(("dp", "gx", "gy"), None),
        P(("dp", "gx", "gy"), None),
        P(("dp", "gx", "gy")),
        P(("dp", "gx", "gy")),
        P(("dp", "gx", "gy")),
        P(("dp", "gx", "gy")),
        P(("dp", "gx", "gy")),
        P(("dp", "gx", "gy")),
        P(("dp", "gx", "gy")),
        P(("dp", "gy"), "gx"),
        P(("dp", "gx", "gy")),
        P(("dp", "gy"), "gx"),
        P(("dp", "gx", "gy")),
    )
    return jax.shard_map(
        per_device,
        mesh=mesh,
        in_specs=placed,
        out_specs=(
            P(("dp", "gx", "gy"), None, None),
            P(("dp", "gx", "gy"), None, None),
            P(("dp", "gx", "gy"), None),
            P(("dp", "gx", "gy"), None),
            P(("dp", "gx", "gy"), None),
            P(("dp", "gx", "gy"), None),
            P(("dp", "gx", "gy")),
            P(("dp", "gx", "gy")),
            P(("dp", "gx", "gy")),
            P(("dp", "gx", "gy")),
            P(("dp", "gx", "gy")),
            P(("dp", "gx", "gy")),
            P(("dp", "gx", "gy")),
            P(("dp", "gy"), "gx"),
            P(("dp", "gx", "gy")),
            P(("dp", "gy"), "gx"),
            P(("dp", "gx", "gy")),
        ),
        check_vma=False,
    )
```

profile of v0, /device:TPU:0, one launch (start us, length us, event | category | flops | bytes accessed | tf_op | source)
XLA Modules:
  0.0 1140.8 jit_solution(7242773581946581646)
XLA Ops:
  12.5 2.0 fusion.67
  16.7 42.7 %all-reduce.19 = (bf16[768]{0:T(1024)(128)(2,1)S(1)}, bf16[768]{0:T(1024)(128)(2,1)S(1)}, bf16[768]{0:T(1024)(128)(2,1)S(1)}, bf16[768]{0:T(1024)(128)(2,1)S(1)}...) all-reduce(bf16[768]{0:T(1024)(128)(2,1)S(1)} %dynamic-update-slice, ...), channel_id=1, replica_groups=mesh['dp'=2,'gx'=4,'gy'=4] {'dp','gx','gy'}, use_global_device_ids=true, to_apply=%add.2 | all-reduce | flops 9216 | bytes 36864
  61.2 6.8 all-gather.11.cloned.1.call-done
  68.0 4.3 add_convert_fusion.4
  72.3 2.7 copy.88
  75.0 48.8 %all-gather.9.cloned.1.call-done = bf16[768,768]{1,0:T(8,128)(2,1)} async-done(((bf16[24,768]{1,0:T(8,128)(2,1)}), bf16[768,768]{1,0:T(8,128)(2,1)}) %all-gather.9.cloned.1.call-update) | async-done | bytes 1179664 | tf_op jit(solution)/shard_map/all_gather | solution.py:102
  123.8 4.8 add_convert_fusion.5
  128.6 3.8 copy.87
  132.4 47.4 %all-gather.13.cloned.1.call-done = bf16[768,768]{1,0:T(8,128)(2,1)} async-done(((bf16[24,768]{1,0:T(8,128)(2,1)}), bf16[768,768]{1,0:T(8,128)(2,1)}) %all-gather.13.cloned.1.call-update) | async-done | bytes 1179664 | tf_op jit(solution)/shard_map/all_gather | solution.py:101
  179.9 4.8 convolution_convert_fusion.3
  184.6 3.9 copy.89
  188.5 62.6 %while.26 = (s32[]{:T(128)}, bf16[2,529,12,64]{1,3,2,0:T(8,128)(2,1)}, f32[2,12,529,1]{2,1,3,0:T(8,128)S(1)}, bf16[2,529,12,64]{1,3,2,0:T(8,128)(2,1)}, s32[2,52...) while((s32[]{:T(128)}, ...), condition=%wide.region_5.6_spmd, body=%wide.region_2.5_spmd.sunk | while | flops 900242112 | bytes 49345764 | solution.py:193
  189.0 9.8 fusion.137
  198.8 9.2 fusion.138
  208.0 11.8 %bitcast_dynamic-update-slice_fusion.4 = bf16[2,529,12,64]{1,3,2,0:T(8,128)(2,1)} fusion(bf16[2,529,12,64]{1,3,2,0:T(8,128)(2,1)} %get-tuple-element.384, s32[]{:T(128)S(6)} %copy.153, f32[12,529,529]{1,2,0:T(8,128)} %get-tuple-element.361, f32[12,529]{1,0:T(8,128)S(1)} %fusion.138, f32[12,529]{1,0:T(8,128)S(1)} %get-tuple-element.362, ...), kind=kOutput, calls=%fused_computation.6.clone.1 | convolution fusion | flops 446626240 | bytes 19405696 | tf_op jit(solution)/shard_map/while/body/eval_jaxpr/hqk,khd->qhd/dot_general | solution.py:54
  220.1 9.8 fusion.137
  229.9 9.3 fusion.138
  239.2 11.9 %bitcast_dynamic-update-slice_fusion.4 = bf16[2,529,12,64]{1,3,2,0:T(8,128)(2,1)} fusion(bf16[2,529,12,64]{1,3,2,0:T(8,128)(2,1)} %get-tuple-element.384, s32[]{:T(128)S(6)} %copy.153, f32[12,529,529]{1,2,0:T(8,128)} %get-tuple-element.361, f32[12,529]{1,0:T(8,128)S(1)} %fusion.138, f32[12,529]{1,0:T(8,128)S(1)} %get-tuple-element.362, ...), kind=kOutput, calls=%fused_computation.6.clone.1 | convolution fusion | flops 446626240 | bytes 19405696 | tf_op jit(solution)/shard_map/while/body/eval_jaxpr/hqk,khd->qhd/dot_general | solution.py:54
  252.4 4.1 fusion.101
  259.9 2.8 copy.91
  263.6 14.1 %all-gather.19.cloned.1.call-done = bf16[768,768]{1,0:T(8,128)(2,1)} async-done(((bf16[96,768]{1,0:T(8,128)(2,1)}), bf16[768,768]{1,0:T(8,128)(2,1)}) %all-gather.19.cloned.1.call-update) | async-done | bytes 1179664 | tf_op jit(solution)/shard_map/all_gather | solution.py:118
  277.7 48.3 %all-gather.17.cloned.1.call-done = bf16[8,529,768]{2,1,0:T(8,128)(2,1)} async-done(((bf16[2,529,768]{2,1,0:T(8,128)(2,1)}), bf16[8,529,768]{2,1,0:T(8,128)(2,1)}) %all-gather.17.cloned.1.call-update) | async-done | bytes 6500368 | tf_op jit(solution)/shard_map/all_gather | solution.py:200
  326.0 21.0 %fusion.71 = (u8[529,768]{1,0:T(8,128)(4,1)S(1)}, u8[529,768]{1,0:T(8,128)(4,1)S(1)}, f32[8,529,768]{2,1,0:T(8,128)S(1)}) fusion(f32[768]{0:T(1024)S(1)} %dynamic-slice_convert_fusion, bf16[8,529,768]{2,1,0:T(8,128)(2,1)} %all-gather.17.cloned.1.call-done, bf16[768,768]{1,0:T(8,128)(2,1)} %all-gather.19.cloned.1.call-done), kind=kOutput, calls=%fused_computation.118 | convolution fusion | flops 5036959744 | bytes 21496320 | tf_op jit(solution)/shard_map/nxt,tp->nxp/dot_general | solution.py:21
  347.0 4.8 copy-done.13
  351.7 31.4 %multiply_convert_fusion.3 = (bf16[8,529,768]{2,1,0:T(8,128)(2,1)}, f32[8,529,768]{2,1,0:T(8,128)}) fusion(f32[8,529,768]{2,1,0:T(8,128)S(1)} %get-tuple-element.257, f32[768]{0:T(1024)S(1)} %dynamic-slice_convert_fusion, u8[529,768]{1,0:T(8,128)(4,1)S(1)} %get-tuple-element.183, u8[529,768]{1,0:T(8,128)(4,1)S(1)} %get-tuple-element.182), kind=kLoop, calls=%fused_computation.67 | loop fusion | flops 230762496 | bytes 33317376 | tf_op jit(solution)/shard_map/convert_element_type | solution.py:204
  383.2 34.4 %all-gather.23.cloned.1.call-done = bf16[8,529,768]{2,1,0:T(8,128)(2,1)} async-done(((bf16[2,529,768]{2,1,0:T(8,128)(2,1)}), bf16[8,529,768]{2,1,0:T(8,128)(2,1)}) %all-gather.23.cloned.1.call-update) | async-done | bytes 6500368 | tf_op jit(solution)/shard_map/all_gather | solution.py:229
  417.6 20.1 %convert_reduce_fusion = (f32[768]{0:T(1024)}, bf16[8,529,768]{2,1,0:T(8,128)(2,1)}) fusion(f32[8,529,768]{2,1,0:T(8,128)} %get-tuple-element.247, bf16[8,529,768]{2,1,0:T(8,128)(2,1)} %all-gather.23.cloned.1.call-done, bf16[768,768]{1,0:T(8,128)(2,1)} %all-gather.21.cloned.1.call-done, f32[8,529,768]{2,1,0:T(8,128)} %copy-done.13, ...), kind=kOutput, calls=%fused_computation.65 | convolution fusion | flops 5047522304 | bytes 40187904 | tf_op jit(solution)/shard_map/nxt,tp->nxp/dot_general | solution.py:230
  437.7 10.6 convolution_convert_fusion
  448.4 10.0 convolution_convert_fusion.1
  458.4 11.4 %convolution_bitcast_fusion = f32[768,768]{0,1:T(8,128)} fusion(bf16[8,529,768]{2,1,0:T(8,128)(2,1)} %get-tuple-element.246, bf16[8,529,768]{2,1,0:T(8,128)(2,1)} %all-gather.23.cloned.1.call-done), kind=kOutput, calls=%fused_computation.122 | convolution fusion | flops 4992270336 | bytes 15360000 | tf_op jit(solution)/shard_map/zvy,zvn->yn/dot_general | solution.py:33
  469.8 3.4 copy.116
  473.3 10.5 convolution_bitcast_fusion.1
  484.0 24.8 %reduce-scatter.13.cloned.1.call-done = bf16[2,529,768]{2,1,0:T(8,128)(2,1)} async-done(((bf16[8,529,768]{2,1,0:T(8,128)(2,1)}), bf16[2,529,768]{2,1,0:T(8,128)(2,1)}) %reduce-scatter.13.cloned.1.call-update) | async-done | bytes 1625104 | tf_op jit(solution)/shard_map/reduce_scatter | solution.py:238
  508.8 3.3 convert_reduce_fusion.1
  512.1 2.5 fusion.69
  514.7 2.1 convert_reduce_fusion.6
  519.6 2.3 copy.93
  521.9 5.5 convolution_bitcast_fusion.2
  527.5 97.8 %while.27 = (s32[]{:T(128)}, bf16[2,529,12,64]{1,3,2,0:T(8,128)(2,1)}, bf16[2,529,12,64]{1,3,2,0:T(8,128)(2,1)}, bf16[2,529,12,64]{1,3,2,0:T(8,128)(2,1)}, bf16[...) while((s32[]{:T(128)}, ...), condition=%wide.region_14.15_spmd, body=%wide.region_12.14_spmd.sunk | while | flops 2181706752 | bytes 172887152 | solution.py:255
  528.1 11.0 subtract_exponential_fusion.3
  539.0 8.6 fusion.149
  547.7 11.2 multiply_reduce_fusion.3
  558.8 11.5 %multiply_convert_fusion.5 = bf16[12,529,529]{1,2,0:T(8,128)(2,1)S(1)} fusion(f32[12,529,529]{1,2,0:T(8,128)} %subtract_exponential_fusion.3, f32[12,529,529]{1,2,0:T(8,128)} %get-tuple-element.373, f32[12,529]{1,0:T(8,128)S(1)} %get-tuple-element.374), kind=kLoop, calls=%fused_computation.21.clone.1 | loop fusion | flops 10074276 | bytes 33606312 | tf_op jit(solution)/shard_map/while/body/eval_jaxpr/convert_element_type | solution.py:69
  570.3 2.8 fusion.148
  576.6 11.0 subtract_exponential_fusion.3
  587.6 8.7 fusion.149
  596.3 11.4 multiply_reduce_fusion.3
  607.7 11.6 %multiply_convert_fusion.5 = bf16[12,529,529]{1,2,0:T(8,128)(2,1)S(1)} fusion(f32[12,529,529]{1,2,0:T(8,128)} %subtract_exponential_fusion.3, f32[12,529,529]{1,2,0:T(8,128)} %get-tuple-element.373, f32[12,529]{1,0:T(8,128)S(1)} %get-tuple-element.374), kind=kLoop, calls=%fused_computation.21.clone.1 | loop fusion | flops 10074276 | bytes 33606312 | tf_op jit(solution)/shard_map/while/body/eval_jaxpr/convert_element_type | solution.py:69
  619.3 2.8 fusion.148
  625.4 6.0 convolution_bitcast_fusion.4
  631.6 5.3 convolution_bitcast_fusion.3
  637.3 5.4 convolution_bitcast_fusion.5
  642.8 5.2 fusion.81
  649.4 3.5 fusion.84
  652.9 2.7 fusion.98
  657.6 41.5 %all-reduce.18 = (f32[768]{0:T(1024)S(1)}, f32[768]{0:T(1024)S(1)}, f32[768]{0:T(1024)S(1)}, f32[768]{0:T(1024)S(1)}, f32[768]{0:T(1024)S(1)}, /*index=5*/f32[76...) all-reduce(f32[768]{0:T(1024)S(1)} %get-tuple-element.186, ...), channel_id=8, replica_groups=mesh['dp'=2,'gx'=4,'gy'=4] {'dp','gx','gy'}, use_global_device_ids=true, to_apply=%region_22.23.clone | all-reduce | flops 9216 | bytes 73728
  703.9 5.6 add_convert_fusion.1
  709.5 2.4 copy.102
  711.9 2.4 copy.101
  714.9 1.9 reduce-scatter.23.cloned.1.call-done
  716.8 104.0 %reduce-scatter.21.cloned.1.call-done = f32[24,768]{1,0:T(8,128)} async-done(((f32[768,768]{1,0:T(8,128)}), f32[24,768]{1,0:T(8,128)}) %reduce-scatter.21.cloned.1.call-update) | async-done | bytes 73744 | tf_op jit(solution)/shard_map/reduce_scatter | solution.py:285
  820.8 104.6 %reduce-scatter.17.cloned.1.call-done = f32[24,768]{1,0:T(8,128)} async-done(((f32[768,768]{1,0:T(8,128)}), f32[24,768]{1,0:T(8,128)}) %reduce-scatter.17.cloned.1.call-update) | async-done | bytes 73744 | tf_op jit(solution)/shard_map/reduce_scatter | solution.py:283
  925.5 103.8 %reduce-scatter.19.cloned.1.call-done = f32[24,768]{1,0:T(8,128)} async-done(((f32[768,768]{1,0:T(8,128)}), f32[24,768]{1,0:T(8,128)}) %reduce-scatter.19.cloned.1.call-update) | async-done | bytes 73744 | tf_op jit(solution)/shard_map/reduce_scatter | solution.py:284
  1029.2 104.6 %reduce-scatter.15.cloned.1.call-done = f32[24,768]{1,0:T(8,128)} async-done(((f32[768,768]{1,0:T(8,128)}), f32[24,768]{1,0:T(8,128)}) %reduce-scatter.15.cloned.1.call-update) | async-done | bytes 73744 | tf_op jit(solution)/shard_map/reduce_scatter | solution.py:282
  (262 shorter events, 33.8 us)
Async XLA Ops:
  7.2 60.8 %copy-start.6 = (bf16[2,529,768]{2,0,1:T(2,128)(2,1)S(1)}, bf16[2,529,768]{2,0,1:T(2,128)(2,1)}, u32[]{:S(2)}) copy-start(bf16[2,529,768]{2,0,1:T(2,128)(2,1)} %param.22) | copy-start | bytes 4875268
  7.2 7.4 copy-start.59
  7.2 7.6 copy-start.60
  7.2 7.8 copy-start.61
  7.2 8.1 copy-start.62
  7.2 8.3 copy-start.63
  7.3 8.5 copy-start.64
  7.3 8.7 copy-start.65
  7.3 9.0 copy-start.66
  7.3 9.2 copy-start.67
  7.3 60.7 %all-gather.11.cloned.1.call-start = ((), (), s32[]{:S(2)}) async-start(), calls=%async_computation.9 | async-start | bytes 1216512 | tf_op jit(solution)/shard_map/all_gather | solution.py:100
  8.0 115.8 %all-gather.9.cloned.1.call-start = ((), (), s32[]{:S(2)}) async-start(), calls=%async_computation.8 | async-start | bytes 1216512 | tf_op jit(solution)/shard_map/all_gather | solution.py:102
  8.8 171.1 %all-gather.13.cloned.1.call-start = ((), (), s32[]{:S(2)}) async-start(), calls=%async_computation.10 | async-start | bytes 1216512 | tf_op jit(solution)/shard_map/all_gather | solution.py:101
  9.5 241.6 %all-gather.15.cloned.1.call-start = ((), (), s32[]{:S(2)}) async-start(), calls=%async_computation.11 | async-start | bytes 1216512 | tf_op jit(solution)/shard_map/all_gather | solution.py:103
  10.1 267.6 %all-gather.19.cloned.1.call-start = ((), (), s32[]{:S(2)}) async-start(), calls=%async_computation.13 | async-start | bytes 1327104 | tf_op jit(solution)/shard_map/all_gather | solution.py:118
  10.7 315.3 %all-gather.17.cloned.1.call-start = ((), (), s32[]{:S(2)}) async-start(), calls=%async_computation.12 | async-start | bytes 8232960 | tf_op jit(solution)/shard_map/all_gather | solution.py:200
  12.5 167.4 %copy-start.26 = (f32[2,529]{1,0:T(2,128)}, f32[2,529]{1,0:T(2,128)S(1)}, u32[]{:S(2)}) copy-start(f32[2,529]{1,0:T(2,128)S(1)} %broadcast_multiply_fusion.1) | copy-start | bytes 12700
  14.5 53.5 %copy-start.41 = (f32[2,529]{1,0:T(2,128)}, f32[2,529]{1,0:T(2,128)S(1)}, u32[]{:S(2)}) copy-start(f32[2,529]{1,0:T(2,128)S(1)} %fusion.67) | copy-start | bytes 12700
  14.5 165.3 %copy-start.37 = (f32[2,529]{1,0:T(2,128)}, f32[2,529]{1,0:T(2,128)S(1)}, u32[]{:S(2)}) copy-start(f32[2,529]{1,0:T(2,128)S(1)} %fusion.89) | copy-start | bytes 12700
  59.4 120.5 %copy-start.33 = (f32[768]{0:T(1024)}, f32[768]{0:T(1024)S(1)}, u32[]{:S(2)}) copy-start(f32[768]{0:T(1024)S(1)} %convert_element_type.127) | copy-start | bytes 9220
  59.4 120.4 %copy-start.48 = (f32[768]{0:T(1024)}, f32[768]{0:T(1024)S(1)}, u32[]{:S(2)}) copy-start(f32[768]{0:T(1024)S(1)} %convert_element_type.128) | copy-start | bytes 9220
  188.5 63.9 %copy-start.50 = (f32[768]{0:T(1024)S(1)}, f32[768]{0:T(1024)}, u32[]{:S(2)}) copy-start(f32[768]{0:T(1024)} %convert_element_type.137) | copy-start | bytes 9220
  256.5 258.2 %copy-start = (f32[2,529,768]{2,1,0:T(8,128)}, f32[2,529,768]{2,1,0:T(8,128)S(1)}, u32[]{:S(2)}) copy-start(f32[2,529,768]{2,1,0:T(8,128)S(1)} %get-tuple-element.256) | copy-start | bytes 9750532
  256.5 258.1 %copy-start.24 = (f32[2,529]{1,0:T(2,128)}, f32[2,529]{1,0:T(2,128)S(1)}, u32[]{:S(2)}) copy-start(f32[2,529]{1,0:T(2,128)S(1)} %broadcast_multiply_fusion) | copy-start | bytes 12700
  257.3 257.4 %copy-start.30 = (f32[2,529]{1,0:T(2,128)}, f32[2,529]{1,0:T(2,128)S(1)}, u32[]{:S(2)}) copy-start(f32[2,529]{1,0:T(2,128)S(1)} %fusion.90) | copy-start | bytes 12700
  259.1 124.1 %all-gather.21.cloned.1.call-start = ((), (), s32[]{:S(2)}) async-start(), calls=%async_computation.14 | async-start | bytes 1327104 | tf_op jit(solution)/shard_map/all_gather | solution.py:119
  259.8 157.8 %all-gather.23.cloned.1.call-start = ((), (), s32[]{:S(2)}) async-start(), calls=%async_computation.16 | async-start | bytes 8232960 | tf_op jit(solution)/shard_map/all_gather | solution.py:229
  262.7 246.1 %reduce-scatter.13.cloned.1.call-start = ((), (), s32[]{:S(2)}) async-start(), calls=%async_computation.17 | async-start | bytes 8232960 | tf_op jit(solution)/shard_map/reduce_scatter | solution.py:238
  347.0 4.8 copy-start.13
  417.6 20.1 %copy-start.58 = (bf16[768,768]{1,0:T(8,128)(2,1)S(1)}, bf16[768,768]{1,0:T(8,128)(2,1)}, u32[]{:S(2)}) copy-start(bf16[768,768]{1,0:T(8,128)(2,1)} %all-gather.19.cloned.1.call-done) | copy-start | bytes 3538948
  448.3 255.5 %reduce-scatter.11.cloned.1.call-start = ((), (), s32[]{:S(2)}) async-start(), calls=%async_computation.15 | async-start | bytes 8232960 | tf_op jit(solution)/shard_map/reduce_scatter | solution.py:208
  458.4 256.6 %reduce-scatter.25.cloned.1.call-start = ((), (), s32[]{:S(2)}) async-start(), calls=%async_computation.23 | async-start | bytes 2654208
  473.3 243.5 %reduce-scatter.23.cloned.1.call-start = ((), (), s32[]{:S(2)}) async-start(), calls=%async_computation.22 | async-start | bytes 2654208 | tf_op jit(solution)/shard_map/reduce_scatter | solution.py:245
  483.9 336.9 %reduce-scatter.21.cloned.1.call-start = ((), (), s32[]{:S(2)}) async-start(), calls=%async_computation.21 | async-start | bytes 2433024 | tf_op jit(solution)/shard_map/reduce_scatter | solution.py:285
  521.9 5.6 copy-start.3
  527.4 398.0 %reduce-scatter.17.cloned.1.call-start = ((), (), s32[]{:S(2)}) async-start(), calls=%async_computation.19 | async-start | bytes 2433024 | tf_op jit(solution)/shard_map/reduce_scatter | solution.py:283
  527.5 97.9 %copy-start.27 = (f32[2,529]{1,0:T(2,128)S(1)}, f32[2,529]{1,0:T(2,128)}, u32[]{:S(2)}) copy-start(f32[2,529]{1,0:T(2,128)} %copy-done.26) | copy-start | bytes 12700
  527.5 97.9 %copy-start.34 = (f32[768]{0:T(1024)S(1)}, f32[768]{0:T(1024)}, u32[]{:S(2)}) copy-start(f32[768]{0:T(1024)} %copy-done.33) | copy-start | bytes 9220
  527.5 97.9 %copy-start.38 = (f32[2,529]{1,0:T(2,128)S(1)}, f32[2,529]{1,0:T(2,128)}, u32[]{:S(2)}) copy-start(f32[2,529]{1,0:T(2,128)} %copy-done.37) | copy-start | bytes 12700
  527.5 97.9 %copy-start.49 = (f32[768]{0:T(1024)S(1)}, f32[768]{0:T(1024)}, u32[]{:S(2)}) copy-start(f32[768]{0:T(1024)} %copy-done.48) | copy-start | bytes 9220
  528.0 11.0 copy-start.5
  528.0 11.0 copy-start.14
  539.0 8.6 copy-start.11
  547.6 11.2 copy-start.15
  558.8 11.5 %copy-start.53 = (bf16[2,529,12,64]{1,3,2,0:T(8,128)(2,1)S(1)}, bf16[2,529,12,64]{1,3,2,0:T(8,128)(2,1)}, u32[]{:S(2)}) copy-start(bf16[2,529,12,64]{1,3,2,0:T(8,128)(2,1)} %get-tuple-element.412) | copy-start | bytes 4875268 | tf_op jit(solution)/shard_map/while
  576.5 11.0 copy-start.5
  576.6 11.0 copy-start.14
  587.6 8.7 copy-start.11
  596.3 11.4 %copy-start.15 = (bf16[2,529,12,64]{1,3,2,0:T(8,128)(2,1)}, bf16[2,529,12,64]{1,3,2,0:T(8,128)(2,1)S(1)}, u32[]{:S(2)}) copy-start(bf16[2,529,12,64]{1,3,2,0:T(8,128)(2,1)S(1)} %fusion.149) | copy-start | bytes 4875268 | tf_op jit(solution)/shard_map/while
  607.7 11.6 %copy-start.53 = (bf16[2,529,12,64]{1,3,2,0:T(8,128)(2,1)S(1)}, bf16[2,529,12,64]{1,3,2,0:T(8,128)(2,1)}, u32[]{:S(2)}) copy-start(bf16[2,529,12,64]{1,3,2,0:T(8,128)(2,1)} %get-tuple-element.412) | copy-start | bytes 4875268 | tf_op jit(solution)/shard_map/while
  625.4 6.1 copy-start.7
  631.5 397.7 %reduce-scatter.19.cloned.1.call-start = ((), (), s32[]{:S(2)}) async-start(), calls=%async_computation.20 | async-start | bytes 2433024 | tf_op jit(solution)/shard_map/reduce_scatter | solution.py:284
  631.5 5.4 copy-start.52
  631.6 5.5 copy-start.51
  636.9 496.9 %reduce-scatter.15.cloned.1.call-start = ((), (), s32[]{:S(2)}) async-start(), calls=%async_computation.18 | async-start | bytes 2433024 | tf_op jit(solution)/shard_map/reduce_scatter | solution.py:282
  637.3 5.5 copy-start.56
  642.8 5.3 copy-start.16
  642.8 5.3 copy-start.21
  655.7 48.2 %copy-start.1 = (f32[2,529,768]{2,1,0:T(8,128)S(1)}, f32[2,529,768]{2,1,0:T(8,128)}, u32[]{:S(2)}) copy-start(f32[2,529,768]{2,1,0:T(8,128)} %copy-done) | copy-start | bytes 9750532
  655.7 48.1 %copy-start.25 = (f32[2,529]{1,0:T(2,128)S(1)}, f32[2,529]{1,0:T(2,128)}, u32[]{:S(2)}) copy-start(f32[2,529]{1,0:T(2,128)} %copy-done.24) | copy-start | bytes 12700
  655.7 48.1 %copy-start.29 = (f32[768]{0:T(1024)S(1)}, f32[768]{0:T(1024)}, u32[]{:S(2)}) copy-start(f32[768]{0:T(1024)} %convert_element_type.138) | copy-start | bytes 9220
  655.7 48.1 %copy-start.31 = (f32[2,529]{1,0:T(2,128)S(1)}, f32[2,529]{1,0:T(2,128)}, u32[]{:S(2)}) copy-start(f32[2,529]{1,0:T(2,128)} %copy-done.30) | copy-start | bytes 12700
  655.7 48.1 %copy-start.36 = (f32[2,529]{1,0:T(2,128)S(1)}, f32[2,529]{1,0:T(2,128)}, u32[]{:S(2)}) copy-start(f32[2,529]{1,0:T(2,128)} %copy-done.35) | copy-start | bytes 12700
  655.7 48.1 %copy-start.40 = (f32[2,529]{1,0:T(2,128)S(1)}, f32[2,529]{1,0:T(2,128)}, u32[]{:S(2)}) copy-start(f32[2,529]{1,0:T(2,128)} %copy-done.39) | copy-start | bytes 12700
  (29 other events, 68.8 us)
Sparse Core Ops, SparseCore 0:
  11.0 56.9 all-gather.10
  70.9 52.8 all-gather.8
  126.7 53.0 all-gather.12
  182.6 53.0 all-gather.14
  237.6 39.9 all-gather.18
  279.1 46.8 all-gather.16
  328.0 41.0 all-gather.20
  370.7 46.8 all-gather.22
  448.4 60.3 reduce-scatter.12
  511.3 60.3 reduce-scatter.10
  575.8 69.0 reduce-scatter.24
  648.7 68.0 reduce-scatter.22
  722.7 98.1 reduce-scatter.20
  827.4 98.0 reduce-scatter.16
  931.2 97.9 reduce-scatter.18
  1035.8 98.0 reduce-scatter.14
where the time goes:
time: 1150 us; the launch traced here: 1140 us
  waiting for transfers between devices  648 us (56%)
  matrix products  251 us (22%)
  other arithmetic  98.7 us (9%)
  blocking collectives  84.2 us (7%)
  local copies, waits for them, and re-layouts  42.5 us (4%)
  between operations  15.3 us (1%)
    reduce_scatter x1, waiting for transfers between devices, per_device(): lax.psum_scatter(key_weight_grad, ('dp', 'gx', 'gy'), scatter_dimension=0...  105 us
    reduce_scatter x1, waiting for transfers between devices, per_device(): lax.psum_scatter(query_weight_grad, ('dp', 'gx', 'gy'), scatter_dimension...  105 us
    reduce_scatter x1, waiting for transfers between devices, per_device(): lax.psum_scatter(output_weight_grad, ('dp', 'gx', 'gy'), scatter_dimensio...  104 us
    reduce_scatter x1, waiting for transfers between devices, per_device(): lax.psum_scatter(value_weight_grad, ('dp', 'gx', 'gy'), scatter_dimension...  104 us
    unnamed x2, blocking collectives  84.2 us
    all_gather x1, waiting for transfers between devices, fetch_params(): lax.all_gather(value_weight, ('dp', 'gx', 'gy'), axis=0, tiled=True)  48.8 us
    all_gather x1, waiting for transfers between devices, per_device(): ff_rows = lax.all_gather(second_low, 'gx', axis=0, tiled=True)  48.3 us
    all_gather x1, waiting for transfers between devices, fetch_params(): lax.all_gather(key_weight, ('dp', 'gx', 'gy'), axis=0, tiled=True)  47.4 us
  transfers between devices with their start and end apart: 16, of which 12 were waited for; matrix products, arithmetic and copies ran while one was open for 31% of the time, Pallas kernels for 0%

commit v1 on v0

v1 whole, which is shorter than its diff:
```python
import functools
import math

import jax
import jax.numpy as jnp
from jax import lax
from jax.experimental import pallas as pl
from jax.experimental.pallas import tpu as pltpu
from jax.sharding import PartitionSpec as P

H = 12
HD = 64
BF = jnp.bfloat16
F32 = jnp.float32
ALL = ("dp", "gx", "gy")
MESH = pl.DeviceIdType.MESH
LOG2E = 1.4426950408889634
INV_SQRT2 = 0.7071067811865476
INV_SQRT_2PI = 0.3989422804014327
ANY = pl.BlockSpec(memory_space=pl.ANY)
VM = pl.BlockSpec(memory_space=pltpu.VMEM)
LIMIT = 60 << 20

G1, S1, QB, VB, OB, G2, S2, DB, UB0 = 0, 1, 2, 3, 4, 5, 6, 7, 8


def nn(a, b):
    return lax.dot_general(a, b, (((1,), (0,)), ((), ())), preferred_element_type=F32)


def nt(a, b):
    return lax.dot_general(a, b, (((1,), (1,)), ((), ())), preferred_element_type=F32)


def padded(length):
    return (length + 31) // 32 * 32


def row_pieces(length, step):
    return [(lo, min(step, length - lo)) for lo in range(0, length, step)]


def normalise(rows):
    centred = rows - jnp.mean(rows, axis=-1, keepdims=True)
    scale = lax.rsqrt(jnp.mean(centred * centred, axis=-1, keepdims=True) + 1e-06)
    return centred * scale, scale


def norm_back(grad, gain, xhat, scale):
    t = grad * gain
    return scale * (
        t
        - jnp.mean(t, axis=-1, keepdims=True)
        - xhat * jnp.mean(t * xhat, axis=-1, keepdims=True)
    )


def colsum(rows):
    return jnp.sum(rows, axis=0, keepdims=True)


def place(d, x, g):
    return (d, x, g)


def remote(src, dst, send, recv, dev):
    return pltpu.make_async_remote_copy(
        src_ref=src, dst_ref=dst, send_sem=send, recv_sem=recv, device_id=dev, device_id_type=MESH
    )


def greet(d, x, g, ny):
    h, c = x // 2, x % 2
    barrier = pltpu.get_barrier_semaphore()
    peers = [(d, x, lax.rem(g + k, ny)) for k in range(1, ny)]
    peers += [(1 - d, x, g), (d, (1 - h) * 2 + c, g), (d, h * 2 + 1 - c, g)]
    for peer in peers:
        pl.semaphore_signal(barrier, inc=1, device_id=peer, device_id_type=MESH)
    pl.semaphore_wait(barrier, len(peers))


def block(ref, units_first, d, h, c):
    return ref.at[h, c, d] if units_first else ref.at[d, h, c]


def gather_kernel(orders, ny, *refs):
    n = len(orders)
    shards, outs = refs[:n], refs[n : 2 * n]
    loc, zsend, zrecv, bsend, brecv = refs[2 * n :]
    d, x, g = lax.axis_index("dp"), lax.axis_index("gx"), lax.axis_index("gy")
    h, c = x // 2, x % 2
    greet(d, x, g, ny)
    ydev, xdev, cdev = (d, (1 - h) * 2 + c, g), (1 - d, x, g), (d, h * 2 + 1 - c, g)
    half = ny // 2

    def start_z(t):
        own = block(outs[t], orders[t], d, h, c).at[g]
        local = pltpu.make_async_copy(shards[t], own, loc.at[t])
        local.start()
        copies = []
        for k in range(1, ny):
            dev = (d, x, lax.rem(g + k, ny))
            cp = remote(shards[t], own, zsend.at[t, k - 1], zrecv.at[t, k - 1], dev)
            cp.start()
            copies.append(cp)
        return local, copies

    def start_b(t, zs):
        local, copies = zs
        local.wait()
        for cp in copies:
            cp.wait_recv()
        b = block(outs[t], orders[t], d, h, c)
        res = []
        for i, dev in enumerate((ydev, xdev, cdev)):
            cp = remote(b, b, bsend.at[t, i], brecv.at[t, i], dev)
            cp.start()
            res.append(cp)
        return res

    def start_f(t, bs):
        y, xx, _ = bs
        y.wait_recv()
        by = block(outs[t], orders[t], d, 1 - h, c)
        lo, hi = pl.ds(0, half), pl.ds(half, ny - half)
        f1 = remote(by.at[lo], by.at[lo], bsend.at[t, 3], brecv.at[t, 3], xdev)
        f1.start()
        c1 = remote(by, by, bsend.at[t, 4], brecv.at[t, 4], cdev)
        c1.start()
        xx.wait_recv()
        bx = block(outs[t], orders[t], 1 - d, h, c)
        f2 = remote(bx.at[hi], bx.at[hi], bsend.at[t, 5], brecv.at[t, 5], ydev)
        f2.start()
        c2 = remote(bx, bx, bsend.at[t, 6], brecv.at[t, 6], cdev)
        c2.start()
        return [f1, c1, f2, c2]

    def start_c(t, fs):
        fs[0].wait_recv()
        fs[2].wait_recv()
        bd = block(outs[t], orders[t], 1 - d, 1 - h, c)
        cp = remote(bd, bd, bsend.at[t, 7], brecv.at[t, 7], cdev)
        cp.start()
        return cp

    zs, bs, fs, cs = {}, {}, {}, {}
    for step in range(n + 3):
        if step < n:
            zs[step] = start_z(step)
        if 0 <= step - 1 < n:
            bs[step - 1] = start_b(step - 1, zs[step - 1])
        if 0 <= step - 2 < n:
            fs[step - 2] = start_f(step - 2, bs[step - 2])
        if 0 <= step - 3 < n:
            cs[step - 3] = start_c(step - 3, fs[step - 3])
    for t in range(n):
        for cp in (bs[t][2], fs[t][1], fs[t][3], cs[t]):
            cp.wait_recv()
        for cp in zs[t][1] + bs[t] + fs[t] + [cs[t]]:
            cp.wait_send()


def gather(shards, orders, nd, nh, ny):
    n = len(shards)

    def shape(s, units_first):
        lead = (nh, 2, nd, ny) if units_first else (nd, nh, 2, ny)
        return jax.ShapeDtypeStruct(lead + s.shape, s.dtype)

    return pl.pallas_call(
        functools.partial(gather_kernel, orders, ny),
        out_shape=[shape(s, o) for s, o in zip(shards, orders)],
        in_specs=[ANY] * n,
        out_specs=[ANY] * n,
        scratch_shapes=[
            pltpu.SemaphoreType.DMA((n,)),
            pltpu.SemaphoreType.DMA((n, ny - 1)),
            pltpu.SemaphoreType.DMA((n, ny - 1)),
            pltpu.SemaphoreType.DMA((n, 8)),
            pltpu.SemaphoreType.DMA((n, 8)),
        ],
        compiler_params=pltpu.CompilerParams(collective_id=0, has_side_effects=True),
    )(*shards)


def scatter_kernel(orders, nd, nh, ny, *refs):
    n = len(orders)
    parts, outs = refs[:n], refs[n : 2 * n]
    rest = refs[2 * n :]
    sums, rc, rs, rl, rz = (rest[i * n : (i + 1) * n] for i in range(5))
    lsem, csend, crecv, bsend, brecv, zsend, zrecv = rest[5 * n :]
    d, x, g = lax.axis_index("dp"), lax.axis_index("gx"), lax.axis_index("gy")
    h, c = x // 2, x % 2
    greet(d, x, g, ny)
    ydev, xdev, cdev = (d, (1 - h) * 2 + c, g), (1 - d, x, g), (d, h * 2 + 1 - c, g)
    half = ny // 2
    lo, hi = pl.ds(0, half), pl.ds(half, ny - half)
    quads = [(1 - d, 1 - h), (d, 1 - h), (1 - d, h), (d, h)]

    def start_core(t):
        res = []
        for q, (bd, bh) in enumerate(quads):
            cp = remote(
                block(parts[t], orders[t], bd, bh, 1 - c), rc[t].at[q], csend.at[t, q], crecv.at[t, q], cdev
            )
            cp.start()
            lc = pltpu.make_async_copy(
                block(parts[t], orders[t], bd, bh, c), sums[t].at[q], lsem.at[t, q]
            )
            lc.start()
            res.append((cp, lc))
        return res

    def add(dst, src, lead):
        def body(i, carry):
            dst[i] = (dst[i].astype(F32) + src[i].astype(F32)).astype(dst.dtype)
            return carry

        lax.fori_loop(0, lead, body, 0)

    def start_far(t, cs):
        for q in range(4):
            cs[q][0].wait_recv()
            cs[q][1].wait()
            add(sums[t].at[q], rc[t].at[q], ny)
        a = remote(sums[t].at[0, lo], rs[t].at[0], bsend.at[t, 0], brecv.at[t, 0], xdev)
        b = remote(sums[t].at[0, hi], rs[t].at[1], bsend.at[t, 1], brecv.at[t, 1], ydev)
        a.start()
        b.start()
        return a, b

    def start_near(t, far):
        far[0].wait_recv()
        add(sums[t].at[1, lo], rs[t].at[0], half)
        y = remote(sums[t].at[1], rl[t].at[0], bsend.at[t, 2], brecv.at[t, 2], ydev)
        y.start()
        far[1].wait_recv()
        add(sums[t].at[2, hi], rs[t].at[1], half)
        xx = remote(sums[t].at[2], rl[t].at[1], bsend.at[t, 3], brecv.at[t, 3], xdev)
        xx.start()
        return y, xx

    def start_z(t, near):
        for i in range(2):
            near[i].wait_recv()
            add(sums[t].at[3], rl[t].at[i], ny)
        res = []
        for k in range(1, ny):
            to = lax.rem(g + k, ny)
            cp = remote(
                sums[t].at[3, to], rz[t].at[k - 1], zsend.at[t, k - 1], zrecv.at[t, k - 1], (d, x, to)
            )
            cp.start()
            res.append(cp)
        return res

    def finish(t, zs):
        total = sums[t][3, g].astype(F32)
        for k in range(ny - 1):
            zs[k].wait_recv()
            total = total + rz[t][k].astype(F32)
        outs[t][...] = total

    cs, far, near, zs = {}, {}, {}, {}
    for step in range(n + 4):
        if step < n:
            cs[step] = start_core(step)
        if 0 <= step - 1 < n:
            far[step - 1] = start_far(step - 1, cs[step - 1])
        if 0 <= step - 2 < n:
            near[step - 2] = start_near(step - 2, far[step - 2])
        if 0 <= step - 3 < n:
            zs[step - 3] = start_z(step - 3, near[step - 3])
        if 0 <= step - 4 < n:
            finish(step - 4, zs[step - 4])
    for t in range(n):
        for q in range(4):
            cs[t][q][0].wait_send()
        for cp in far[t] + near[t] + tuple(zs[t]):
            cp.wait_send()


def scatter(parts, orders, nd, nh, ny):
    n = len(parts)
    tails = [p.shape[4:] for p in parts]

    def buffers(lead):
        return [pltpu.VMEM(lead + t, p.dtype) for t, p in zip(tails, parts)]

    return pl.pallas_call(
        functools.partial(scatter_kernel, orders, nd, nh, ny),
        out_shape=[jax.ShapeDtypeStruct(t, F32) for t in tails],
        in_specs=[ANY] * n,
        out_specs=[VM] * n,
        scratch_shapes=buffers((4, ny))
        + buffers((4, ny))
        + buffers((2, ny // 2))
        + buffers((2, ny))
        + buffers((ny - 1,))
        + [
            pltpu.SemaphoreType.DMA((n, 4)),
            pltpu.SemaphoreType.DMA((n, 4)),
            pltpu.SemaphoreType.DMA((n, 4)),
            pltpu.SemaphoreType.DMA((n, 4)),
            pltpu.SemaphoreType.DMA((n, 4)),
            pltpu.SemaphoreType.DMA((n, ny - 1)),
            pltpu.SemaphoreType.DMA((n, ny - 1)),
        ],
        compiler_params=pltpu.CompilerParams(
            collective_id=1, has_side_effects=True, vmem_limit_bytes=LIMIT
        ),
    )(*parts)


def qkv_kernel(x_ref, w_ref, v_ref, qkv_ref, n_ref, bias_ref):
    strips, length, width = x_ref.shape
    lp = n_ref.shape[1]
    gain, shift = v_ref[G1 : G1 + 1, :], v_ref[S1 : S1 + 1, :]
    for s in range(strips):
        for lo, size in row_pieces(length, 136):
            xhat, _ = normalise(x_ref[s, lo : lo + size, :].astype(F32))
            n_ref[s, lo : lo + size, :] = (xhat * gain + shift).astype(BF)
        n_ref[s, length:lp, :] = jnp.zeros((lp - length, width), BF)
    bias_ref[0:1, 0:width] = v_ref[QB : QB + 1, :]
    bias_ref[0:1, width : 2 * width] = jnp.zeros((1, width), F32)
    bias_ref[0:1, 2 * width : 3 * width] = v_ref[VB : VB + 1, :]
    step = 256

    def body(i, carry):
        cols = pl.ds(pl.multiple_of(i * step, step), step)
        w = w_ref[:, cols]
        for s in range(strips):
            qkv_ref[s, :, cols] = (nn(n_ref[s], w) + bias_ref[0:1, cols]).astype(BF)
        return carry

    lax.fori_loop(0, 3 * width // step, body, 0)


def fill_bias(bias_ref, row, col):
    bias_ref[...] = jnp.where(row == col, 0.0, -1e30).astype(F32)


def attend_kernel(qkv_ref, sr_ref, sc_ref, o_ref, lse_ref, bias_ref):
    strips, lp, width = o_ref.shape
    qrows = lp // 2
    first = lax.broadcasted_iota(jnp.int32, (qrows, 128), 1) < HD
    lane = lax.broadcasted_iota(jnp.int32, (qrows, 128), 1)
    scale = 0.125 * LOG2E
    for s in range(strips):
        fill_bias(bias_ref, sc_ref[s], sr_ref[s])
        lse_ref[s] = jnp.zeros((lp, 128), F32)

        def body(p, carry):
            cq = pl.ds(pl.multiple_of(p * 128, 128), 128)
            ck = pl.ds(pl.multiple_of(width + p * 128, 128), 128)
            cv = pl.ds(pl.multiple_of(2 * width + p * 128, 128), 128)
            k, v = qkv_ref[s, :, ck], qkv_ref[s, :, cv]
            for part in range(2):
                rows = pl.ds(part * qrows, qrows)
                q = qkv_ref[s, rows, cq]
                lse = lse_ref[s, rows, :]
                res = []
                for j in range(2):
                    keep = first if j == 0 else jnp.logical_not(first)
                    z = nt(jnp.where(keep, q, jnp.zeros_like(q)), k) * scale + bias_ref[rows, :]
                    top = jnp.max(z, axis=-1, keepdims=True)
                    e = jnp.exp2(z - top)
                    total = jnp.sum(e, axis=-1, keepdims=True)
                    res.append(nn(e.astype(BF), v) / total)
                    lse = jnp.where(lane == 2 * p + j, top + jnp.log2(total), lse)
                o_ref[s, rows, cq] = jnp.where(first, res[0], res[1]).astype(BF)
                lse_ref[s, rows, :] = lse
            return carry

        lax.fori_loop(0, H // 2, body, 0)


def transpose_into(dst_ref, src_ref, lp):
    strips, _, width = src_ref.shape
    for s in range(strips):

        def body(i, carry):
            cols = pl.ds(pl.multiple_of(i * 128, 128), 128)
            dst_ref[s, cols, :] = src_ref[s, :, cols].astype(F32).T.astype(BF)
            return carry

        lax.fori_loop(0, width // 128, body, 0)


def ff_kernel(
    x_ref, mix_ref, dout_in_ref, wo_ref, up_ref, down_ref, v_ref,
    y_ref, rg_ref, mg_ref, gup_ref, gdown_ref, gwo_ref, gv_ref,
    dout_ref, doutT_ref, sec_ref, secT_ref, res_ref, acc_ref, sg_ref, hid_ref, pre_ref,
):
    strips, length, width = x_ref.shape
    lp = mix_ref.shape[1]
    groups = up_ref.shape[0]
    units = up_ref.shape[2]
    gv_ref[...] = jnp.zeros(gv_ref.shape, F32)
    bias_o, gain, shift = v_ref[OB : OB + 1, :], v_ref[G2 : G2 + 1, :], v_ref[S2 : S2 + 1, :]
    step = 256
    for s in range(strips):
        dout_ref[s, 0:length, :] = dout_in_ref[s]
        dout_ref[s, length:lp, :] = jnp.zeros((lp - length, width), BF)

        def proj(i, carry):
            cols = pl.ds(pl.multiple_of(i * step, step), step)
            acc_ref[s, :, cols] = nn(mix_ref[s], wo_ref[:, cols])
            return carry

        lax.fori_loop(0, width // step, proj, 0)
        for lo, size in row_pieces(length, 136):
            rows = pl.ds(lo, size)
            residual = x_ref[s, rows, :].astype(F32) + (acc_ref[s, rows, :] + bias_o)
            res_ref[s, rows, :] = residual
            xhat, _ = normalise(residual)
            sec_ref[s, rows, :] = (xhat * gain + shift).astype(BF)
            acc_ref[s, rows, :] = residual + v_ref[DB : DB + 1, :]
        sec_ref[s, length:lp, :] = jnp.zeros((lp - length, width), BF)
        res_ref[s, length:lp, :] = jnp.zeros((lp - length, width), F32)
        gv_ref[DB : DB + 1, :] += colsum(dout_in_ref[s].astype(F32))
    sg_ref[...] = jnp.zeros(sg_ref.shape, F32)
    transpose_into(doutT_ref, dout_ref, lp)
    transpose_into(secT_ref, sec_ref, lp)

    def group(gi, carry):
        def hidden(i, carry):
            cols = pl.ds(pl.multiple_of(i * step, step), step)
            up, down = up_ref[gi, :, cols], down_ref[gi, :, cols]
            ub = v_ref[pl.ds(UB0 + gi, 1), cols]
            total = jnp.zeros((1, step), F32)
            for s in range(strips):
                pre = nn(sec_ref[s], up) + ub
                hg = nn(dout_ref[s], down)
                cdf = 0.5 + 0.5 * lax.erf(pre * INV_SQRT2)
                pdf = jnp.exp(-0.5 * pre * pre) * INV_SQRT_2PI
                hid_ref[s, :, cols] = (pre * cdf).astype(BF)
                pg = (hg * (cdf + pre * pdf)).astype(BF)
                pre_ref[s, :, cols] = pg
                total = total + colsum(pg.astype(F32))
            gv_ref[pl.ds(UB0 + gi, 1), cols] = total
            return carry

        lax.fori_loop(0, units // step, hidden, 0)

        def back(i, carry):
            rows = pl.ds(pl.multiple_of(i * step, step), step)
            for s in range(strips):
                acc_ref[s, :, rows] += nt(hid_ref[s], down_ref[gi, rows, :])
                sg_ref[s, :, rows] += nt(pre_ref[s], up_ref[gi, rows, :])
            gd = nn(doutT_ref[0, rows, :], hid_ref[0])
            gu = nn(secT_ref[0, rows, :], pre_ref[0])
            for s in range(1, strips):
                gd = gd + nn(doutT_ref[s, rows, :], hid_ref[s])
                gu = gu + nn(secT_ref[s, rows, :], pre_ref[s])
            gdown_ref[gi, rows, :] = gd.astype(BF)
            gup_ref[gi, rows, :] = gu.astype(BF)
            return carry

        lax.fori_loop(0, width // step, back, 0)
        return carry

    lax.fori_loop(0, groups, group, 0)
    for s in range(strips):
        for lo, size in row_pieces(length, 136):
            rows = pl.ds(lo, size)
            y_ref[s, rows, :] = acc_ref[s, rows, :].astype(BF)
            xhat, scale = normalise(res_ref[s, rows, :])
            grad = sg_ref[s, rows, :]
            gv_ref[G2 : G2 + 1, :] += colsum(grad * xhat)
            gv_ref[S2 : S2 + 1, :] += colsum(grad)
            rg = dout_ref[s, rows, :].astype(F32) + norm_back(grad, gain, xhat, scale)
            rg_ref[s, rows, :] = rg
            low = rg.astype(BF)
            sec_ref[s, rows, :] = low
            gv_ref[OB : OB + 1, :] += colsum(low.astype(F32))
        sec_ref[s, length:lp, :] = jnp.zeros((lp - length, width), BF)
        rg_ref[s, length:lp, :] = jnp.zeros((lp - length, width), F32)
    transpose_into(secT_ref, mix_ref, lp)

    def last(i, carry):
        rows = pl.ds(pl.multiple_of(i * step, step), step)
        for s in range(strips):
            mg_ref[s, :, rows] = nt(sec_ref[s], wo_ref[rows, :]).astype(BF)
        gw = nn(secT_ref[0, rows, :], sec_ref[0])
        for s in range(1, strips):
            gw = gw + nn(secT_ref[s, rows, :], sec_ref[s])
        gwo_ref[rows, :] = gw.astype(BF)
        return carry

    lax.fori_loop(0, width // step, last, 0)


def attend_back_kernel(
    qkv_ref, mg_ref, mix_ref, lse_ref, sr_ref, sc_ref, dqkv_ref, bias_ref, lt_ref, dt_ref, kt_ref
):
    strips, lp, width = mg_ref.shape
    krows = lp // 2
    first = lax.broadcasted_iota(jnp.int32, (krows, 128), 1) < HD
    scale = 0.125 * LOG2E
    heads = lax.broadcasted_iota(jnp.int32, (16, width), 0)
    owner = lax.broadcasted_iota(jnp.int32, (16, width), 1) // HD
    pick = jnp.where(heads == owner, 1.0, 0.0).astype(BF)
    for s in range(strips):
        fill_bias(bias_ref, sc_ref[s], sr_ref[s])
        lt_ref[...] = lse_ref[s].T
        prod = mg_ref[s].astype(F32) * mix_ref[s].astype(F32)
        high = prod.astype(BF)
        rest = (prod - high.astype(F32)).astype(BF)
        dt_ref[...] = nt(pick, high) + nt(pick, rest)

        def body(p, carry):
            cq = pl.ds(pl.multiple_of(p * 128, 128), 128)
            ck = pl.ds(pl.multiple_of(width + p * 128, 128), 128)
            cv = pl.ds(pl.multiple_of(2 * width + p * 128, 128), 128)
            q, do = qkv_ref[s, :, cq], mg_ref[s, :, cq]
            kt_ref[...] = qkv_ref[s, :, ck].astype(F32).T.astype(BF)
            dq = [jnp.zeros((HD, lp), F32), jnp.zeros((HD, lp), F32)]
            for part in range(2):
                rows = pl.ds(part * krows, krows)
                k, v = qkv_ref[s, rows, ck], qkv_ref[s, rows, cv]
                dv, dk = [], []
                for j in range(2):
                    keep = first if j == 0 else jnp.logical_not(first)
                    lse = lt_ref[pl.ds(2 * p + j, 1), :]
                    delta = dt_ref[pl.ds(2 * p + j, 1), :]
                    z = nt(jnp.where(keep, k, jnp.zeros_like(k)), q) * scale + bias_ref[rows, :]
                    prob = jnp.exp2(z - lse)
                    pg = nt(jnp.where(keep, v, jnp.zeros_like(v)), do)
                    sg = (prob * (pg - delta)).astype(BF)
                    dv.append(nn(prob.astype(BF), do))
                    dk.append(nn(sg, q))
                    dq[j] = dq[j] + nn(kt_ref[j * HD : (j + 1) * HD, part * krows : (part + 1) * krows], sg)
                dqkv_ref[s, rows, cv] = jnp.where(first, dv[0], dv[1]).astype(BF)
                dqkv_ref[s, rows, ck] = (0.125 * jnp.where(first, dk[0], dk[1])).astype(BF)
            dqkv_ref[s, :, cq] = (0.125 * jnp.concatenate(dq, axis=0)).T.astype(BF)
            return carry

        lax.fori_loop(0, H // 2, body, 0)


def qkv_back_kernel(
    x_ref, n_ref, dqkv_ref, rg_ref, w_ref, v_ref, gx_ref, gw_ref, gv_ref, nT_ref, ng_ref
):
    strips, length, width = x_ref.shape
    lp = n_ref.shape[1]
    step = 256
    gv_ref[...] = jnp.zeros(gv_ref.shape, F32)
    gain = v_ref[G1 : G1 + 1, :]
    transpose_into(nT_ref, n_ref, lp)
    for s in range(strips):
        gv_ref[QB : QB + 1, :] += colsum(dqkv_ref[s, :, 0:width].astype(F32))
        gv_ref[VB : VB + 1, :] += colsum(dqkv_ref[s, :, 2 * width : 3 * width].astype(F32))

        def body(i, carry):
            rows = pl.ds(pl.multiple_of(i * step, step), step)
            ng_ref[s, :, rows] = nt(dqkv_ref[s], w_ref[rows, :])
            return carry

        lax.fori_loop(0, width // step, body, 0)

    def grads(i, carry):
        cols = pl.ds(pl.multiple_of(i * step, step), step)
        gw = nn(nT_ref[0], dqkv_ref[0, :, cols])
        for s in range(1, strips):
            gw = gw + nn(nT_ref[s], dqkv_ref[s, :, cols])
        gw_ref[:, cols] = gw.astype(BF)
        return carry

    lax.fori_loop(0, 3 * width // step, grads, 0)
    for s in range(strips):
        for lo, size in row_pieces(length, 136):
            rows = pl.ds(lo, size)
            xhat, scale = normalise(x_ref[s, rows, :].astype(F32))
            grad = ng_ref[s, rows, :]
            gv_ref[G1 : G1 + 1, :] += colsum(grad * xhat)
            gv_ref[S1 : S1 + 1, :] += colsum(grad)
            term = norm_back(grad, gain, xhat, scale)
            gx_ref[s, rows, :] = (rg_ref[s, rows, :] + term).astype(BF)


def call(kernel, outs, n_in, scratch=()):
    return pl.pallas_call(
        kernel,
        out_shape=outs,
        in_specs=[VM] * n_in,
        out_specs=[VM] * len(outs),
        scratch_shapes=list(scratch),
        compiler_params=pltpu.CompilerParams(vmem_limit_bytes=LIMIT),
    )


def sds(shape, dtype):
    return jax.ShapeDtypeStruct(shape, dtype)


def per_device(
    sizes, block_input, segment_ids, out_grad, query_weight, key_weight, value_weight, output_weight,
    first_gain, first_shift, query_bias, value_bias, output_bias, second_gain, second_shift,
    up_weight, up_bias, down_weight, down_bias,
):
    nd, nx, ny = sizes
    n_dev = nd * nx * ny
    strips, length, width = block_input.shape
    lp = padded(length)
    units = up_weight.shape[1]
    att_rows, ff_rows = query_weight.shape[0], up_weight.shape[0]
    own = nd == 2 and nx == 4 and att_rows % 8 == 0 and ff_rows % 8 == 0

    att = jnp.concatenate([query_weight, key_weight, value_weight, output_weight], axis=1)
    vecs = [first_gain, first_shift, query_bias, value_bias, output_bias, second_gain, second_shift, down_bias]
    n_vec = len(vecs)
    small = jnp.concatenate(vecs + [up_bias])
    n_small = small.shape[0]
    lanes = (n_small + 127) // 128
    small = jnp.pad(small.astype(F32), (0, lanes * 128 - n_small)).reshape(lanes, 128)
    if own:
        att, up, down, small = gather(
            [att, up_weight, down_weight, small], [False, True, True, False], nd, nx // 2, ny
        )
    else:
        att, small = (lax.all_gather(a, ALL, axis=0) for a in (att, small))
        up, down = (
            lax.all_gather(lax.all_gather(a, ("dp", "gy"), axis=0), "gx", axis=0)
            for a in (up_weight, down_weight)
        )
    att = att.reshape(width, 4 * width)
    up, down = up.reshape(nx, width, units), down.reshape(nx, width, units)
    small = small.reshape(n_dev, lanes * 128)
    cut = n_vec * att_rows
    table = small[:, :cut].reshape(n_dev, n_vec, att_rows).transpose(1, 0, 2).reshape(n_vec, width)
    table = jnp.concatenate([table, small[:, cut:n_small].reshape(-1, width)])
    w_qkv, w_out = att[:, : 3 * width], att[:, 3 * width :]

    seg = jnp.pad(segment_ids, ((0, 0), (0, lp - length)), constant_values=-1)
    seg_row, seg_col = seg[:, None, :], seg[:, :, None]
    full = (strips, lp, width)
    wide = (strips, lp, 3 * width)
    turned = (strips, width, lp)
    qkv, normed = call(
        qkv_kernel, [sds(wide, BF), sds(full, BF)], 3, [pltpu.VMEM((8, 3 * width), F32)]
    )(block_input, w_qkv, table)
    mixed, lse = call(
        attend_kernel, [sds(full, BF), sds((strips, lp, 128), F32)], 3, [pltpu.VMEM((lp, lp), F32)]
    )(qkv, seg_row, seg_col)
    n_tab = table.shape[0]
    y, res_grad, mixed_grad, g_up, g_down, g_out, g_tab = call(
        ff_kernel,
        [
            sds(block_input.shape, BF), sds(full, F32), sds(full, BF), sds(up.shape, BF),
            sds(down.shape, BF), sds((width, width), BF), sds((n_tab, width), F32),
        ],
        7,
        [
            pltpu.VMEM(full, BF), pltpu.VMEM(turned, BF), pltpu.VMEM(full, BF), pltpu.VMEM(turned, BF),
            pltpu.VMEM(full, F32), pltpu.VMEM(full, F32), pltpu.VMEM(full, F32),
            pltpu.VMEM((strips, lp, units), BF), pltpu.VMEM((strips, lp, units), BF),
        ],
    )(block_input, mixed, out_grad, w_out, up, down, table)
    (dqkv,) = call(
        attend_back_kernel,
        [sds(wide, BF)],
        6,
        [
            pltpu.VMEM((lp, lp), F32), pltpu.VMEM((128, lp), F32), pltpu.VMEM((16, lp), F32),
            pltpu.VMEM((128, lp), BF),
        ],
    )(qkv, mixed_grad, mixed, lse, seg_row, seg_col)
    x_grad, g_qkv, g_tab1 = call(
        qkv_back_kernel,
        [sds(block_input.shape, BF), sds((width, 3 * width), BF), sds((n_tab, width), F32)],
        6,
        [pltpu.VMEM(turned, BF), pltpu.VMEM(full, F32)],
    )(block_input, normed, dqkv, res_grad, w_qkv, table)

    g_tab = g_tab + g_tab1
    g_small = jnp.concatenate(
        [
            g_tab[:n_vec].reshape(n_vec, n_dev, att_rows).transpose(1, 0, 2).reshape(n_dev, cut),
            g_tab[n_vec:].reshape(n_dev, n_small - cut),
        ],
        axis=1,
    )
    g_small = jnp.pad(g_small, ((0, 0), (0, lanes * 128 - n_small)))
    if own:
        nh = nx // 2
        g_qkv, g_out, g_up, g_down, g_small = scatter(
            [
                g_qkv.reshape(nd, nh, 2, ny, att_rows, 3 * width),
                g_out.reshape(nd, nh, 2, ny, att_rows, width),
                g_up.reshape(nh, 2, nd, ny, ff_rows, units),
                g_down.reshape(nh, 2, nd, ny, ff_rows, units),
                g_small.reshape(nd, nh, 2, ny, lanes, 128),
            ],
            [False, False, True, True, False],
            nd,
            nh,
            ny,
        )
    else:
        g_qkv, g_out, g_small = (
            lax.psum_scatter(a.astype(F32), ALL, scatter_dimension=0, tiled=True)
            for a in (g_qkv, g_out, g_small)
        )
        gx = lax.axis_index("gx")
        g_up, g_down = (
            lax.psum_scatter(
                lax.psum_scatter(a.astype(F32), "gx", scatter_dimension=0, tiled=True)[0],
                ("dp", "gy"),
                scatter_dimension=0,
                tiled=True,
            )
            for a in (g_up, g_down)
        )
    g_small = g_small.reshape(lanes * 128)
    gv = [g_small[i * att_rows : (i + 1) * att_rows] for i in range(n_vec)]
    return (
        y,
        x_grad,
        g_qkv[:, :width],
        g_qkv[:, width : 2 * width],
        g_qkv[:, 2 * width :],
        g_out,
        gv[G1],
        gv[S1],
        gv[QB],
        gv[VB],
        gv[OB],
        gv[G2],
        gv[S2],
        g_up,
        g_small[cut:n_small],
        g_down,
        gv[DB],
    )


def solution(mesh):
    rows, cols = P(ALL, None), P(ALL)
    cube = P(ALL, None, None)
    ff = P(("dp", "gy"), "gx")
    sizes = (mesh.shape["dp"], mesh.shape["gx"], mesh.shape["gy"])
    return jax.shard_map(
        functools.partial(per_device, sizes),
        mesh=mesh,
        in_specs=(cube, rows, cube) + (rows,) * 4 + (cols,) * 7 + (ff, cols, ff, cols),
        out_specs=(cube, cube) + (rows,) * 4 + (cols,) * 7 + (ff, cols, ff, cols),
        check_vma=False,
    )
```

time: 1150 us -> 371 us (0.32)
  waiting for transfers between devices: 648 us -> 0 us
  Pallas kernels: 0 us -> 331 us
  matrix products: 251 us -> 0 us
  other arithmetic: 98.7 us -> 2.16 us
  blocking collectives: 84.2 us -> 0 us
  between operations: 15.3 us -> 0.77 us
    reduce_scatter x7 -> x0, waiting for transfers between devices: 444 us -> none  [the longest x1 105 us: per_device(): lax.psum_scatter(key_weight_grad, ('dp', 'gx', 'gy'), scatter_dimension=0...]
    pallas_call x0 -> x7, Pallas kernels: none -> 331 us  [the longest x1 86.2 us: scatter(): pl.pallas_call(functools.partial(scatter_kernel, orders, nd, nh, ny), out...]
    dot_general x32 -> x0, matrix products: 251 us -> none  [the longest x6 44.3 us: weight_grad(): jnp.einsum('zvy,zvn->yn', input_reduced, gradient_reduced, preferred_elem...]
    all_gather x8 -> x0, waiting for transfers between devices: 200 us -> none  [the longest x1 48.8 us: fetch_params(): lax.all_gather(value_weight, ('dp', 'gx', 'gy'), axis=0, tiled=True)]
    unnamed x2 -> x0, blocking collectives: 84.2 us -> none
    convert_element_type x14 -> x0, other arithmetic: 64.4 us -> none  [the longest x1 31.4 us: per_device(): hidden_reduced = hidden_act.astype(jnp.bfloat16)]
    reduce_sum x10 -> x0, other arithmetic: 33.1 us -> none  [the longest x2 18.5 us: attend_strip(): totals = jnp.sum(exp_rows, axis=-1, keepdims=True)]
    convert_element_type x4 -> x0, local copies, waits for them, and re-layouts: 12.7 us -> none  [the longest x1 3.85 us: per_device(): key_low = project(normed_low, key_full).astype(jnp.bfloat16)]
  transfers between devices with their start and end apart: 16 -> 0, of which waited for: 12 -> 0; matrix products, arithmetic and copies ran while one was open for 31% -> 0% of each run, Pallas kernels for 0% -> 0%
where the time goes in v1:
time: 371 us; the launch traced here: 370 us
  Pallas kernels  331 us (89%)
  local copies, waits for them, and re-layouts  35.7 us (10%)
    pallas_call x1, Pallas kernels, scatter(): pl.pallas_call(functools.partial(scatter_kernel, orders, nd, nh, ny), out...  86.2 us
    pallas_call x1, Pallas kernels, gather(): pl.pallas_call(functools.partial(gather_kernel, orders, ny), out_shape=[s...  82.3 us
    pallas_call x1, Pallas kernels, per_device(): call(ff_kernel, [sds(block_input.shape, BF), sds(full, F32), sds(full, BF...  70.1 us
    pallas_call x1, Pallas kernels, per_device(): call(attend_back_kernel, [sds(wide, BF)], 6, [pltpu.VMEM((lp, lp), F32),...  35.3 us
    pallas_call x1, Pallas kernels, per_device(): call(qkv_back_kernel, [sds(block_input.shape, BF), sds((width, 3 * width)...  23.4 us
    pallas_call x1, Pallas kernels, per_device(): call(attend_kernel, [sds(full, BF), sds((strips, lp, 128), F32)], 3, [plt...  22.4 us
    unnamed x21, local copies, waits for them, and re-layouts  15 us
    pallas_call x1, Pallas kernels, per_device(): call(qkv_kernel, [sds(wide, BF), sds(full, BF)], 3, [pltpu.VMEM((8, 3 * w...  11.6 us

profile of v1, /device:TPU:0, one launch (start us, length us, event | category | flops | bytes accessed | tf_op | source)
XLA Modules:
  0.0 369.9 jit_solution(12828842523380376088)
XLA Ops:
  0.7 6.1 %concatenate.13 = bf16[288]{0:T(512)(128)(2,1)S(1)} concatenate(bf16[24]{0:T(256)(128)(2,1)} %param.25, bf16[24]{0:T(256)(128)(2,1)} %param.26, bf16[24]{0:T(256)(128)(2,1)} %param.27, bf16[24]{0:T(256)(128)(2,1)} %param.28, bf16[24]{0:T(256)(128)(2,1)} %param.29, bf16[24]{0:T(256)(128)(2,1)} %param.30, bf16[24]{0:T(256)(128)(2,1)} %param.31, bf16[24]{0:T(256)(128)(2,1)} %param.35, ...), dimensions={0} | concatenate | bytes 1152 | tf_op jit(solution)/shard_map/concatenate | solution.py:613
  6.8 0.6 bitcast_convert_fusion.refs_3_
  7.3 0.7 pad_bitcast_fusion
  8.0 0.6 broadcast_in_dim.6.sr_ref
  8.6 1.5 pad_maximum_fusion.refs_0_
  10.1 1.0 copy.47.sc_ref
  11.2 0.0 copy-start.2
  11.2 3.0 copy.48.x_ref
  14.1 0.0 copy-done.2
  14.1 1.4 copy.49.dout_in_ref
  15.5 82.3 %shard_map.305 = (bf16[2,2,2,4,24,3072]{5,4,3,2,1,0:T(8,128)(2,1)}, bf16[2,2,2,4,96,768]{5,4,3,2,1,0:T(8,128)(2,1)}, bf16[2,2,2,4,96,768]{5,4,3,2,1,0:T(8,128)(2,1)}, f32[2,2,2,4,3,128]{5,4,3,2,1,0:T(4,128)}) custom-call(bf16[24,3072]{1,0:T(8,128)(2,1)} %pad_maximum_fusion.refs_0_, bf16[96,768]{1,0:T(8,128)(2,1)} %refs_1_.1, bf16[96,768]{1,0:T(8,128)(2,1)} %refs_2_.1, ...), custom_call_target="tpu_custom_call" | custom-call | tf_op jit(solution)/shard_map/pallas_call | solution.py:170
  97.8 0.8 copy.57
  98.7 0.1 slice.74
  98.8 0.1 reshape.93
  98.8 0.1 reshape.91
  99.0 0.1 reshape.92
  99.1 0.0 copy-start.3
  99.1 2.4 slice.75.wo_ref
  101.5 4.0 %slice.72.w_ref = bf16[768,2304]{1,0:T(8,128)(2,1)} slice(bf16[768,3072]{1,0:T(8,128)(2,1)} %bitcast.23), slice={[0:768], [0:2304]} | slice | bytes 7077888 | tf_op jit(solution)/shard_map/slice | solution.py:633
  105.5 0.0 copy-done.3
  105.5 11.6 %shard_map.306 = (bf16[2,544,2304]{2,1,0:T(8,128)(2,1)}, bf16[2,544,768]{2,1,0:T(8,128)(2,1)}) custom-call(bf16[2,529,768]{2,1,0:T(8,128)(2,1)} %copy.48.x_ref, bf16[768,2304]{1,0:T(8,128)(2,1)} %slice.72.w_ref, f32[12,768]{1,0:T(8,128)} %copy-done.3), custom_call_target="tpu_custom_call" | custom-call | tf_op jit(solution)/shard_map/pallas_call | solution.py:640
  117.1 22.4 %shard_map.307 = (bf16[2,544,768]{2,1,0:T(8,128)(2,1)}, f32[2,544,128]{2,1,0:T(8,128)}) custom-call(bf16[2,544,2304]{2,1,0:T(8,128)(2,1)} %get-tuple-element.42.qkv_ref, s32[2,1,544]{2,1,0:T(1,128)} %broadcast_in_dim.6.sr_ref, s32[2,544,1]{2,1,0:T(8,128)} %copy.47.sc_ref), custom_call_target="tpu_custom_call" | custom-call | tf_op jit(solution)/shard_map/pallas_call | solution.py:643
  139.5 70.1 %shard_map.308 = (bf16[2,529,768]{2,1,0:T(8,128)(2,1)}, f32[2,544,768]{2,1,0:T(8,128)}, bf16[2,544,768]{2,1,0:T(8,128)(2,1)}, bf16[4,768,768]{2,1,0:T(8,128)(2,1...) custom-call(bf16[2,529,768]{2,1,0:T(8,128)(2,1)} %copy.48.x_ref, ...), custom_call_target="tpu_custom_call" | custom-call | tf_op jit(solution)/shard_map/pallas_call | solution.py:647
  209.6 35.3 %shard_map.309.dqkv_ref = bf16[2,544,2304]{2,1,0:T(8,128)(2,1)} custom-call(bf16[2,544,2304]{2,1,0:T(8,128)(2,1)} %get-tuple-element.42.qkv_ref, bf16[2,544,768]{2,1,0:T(8,128)(2,1)} %get-tuple-element.48.mg_ref, bf16[2,544,768]{2,1,0:T(8,128)(2,1)} %get-tuple-element.43.mix_ref, f32[2,544,128]{2,1,0:T(8,128)} %get-tuple-element.49.lse_ref, ...), custom_call_target="tpu_custom_call" | custom-call | tf_op jit(solution)/shard_map/pallas_call | solution.py:660
  244.9 0.0 copy-start
  244.9 23.4 %shard_map.310 = (bf16[2,529,768]{2,1,0:T(8,128)(2,1)}, bf16[768,2304]{1,0:T(8,128)(2,1)}, f32[12,768]{1,0:T(8,128)}) custom-call(bf16[2,529,768]{2,1,0:T(8,128)(2,1)} %copy.48.x_ref, bf16[2,544,768]{2,1,0:T(8,128)(2,1)} %get-tuple-element.47.n_ref, bf16[2,544,2304]{2,1,0:T(8,128)(2,1)} %shard_map.309.dqkv_ref, f32[2,544,768]{2,1,0:T(8,128)} %get-tuple-element.50.rg_ref, ...), custom_call_target="tpu_custom_call" | custom-call | tf_op jit(solution)/shard_map/pallas_call | solution.py:669
  268.3 0.0 copy-start.4
  268.3 0.0 copy-start.5
  268.3 0.0 copy-done
  268.3 0.0 copy-start.1
  268.4 2.4 copy.53
  270.8 0.0 copy-done.4
  270.8 0.0 copy-done.5
  270.8 0.0 copy-done.1
  270.8 2.4 copy.54
  273.2 0.1 reshape.102
  273.3 0.1 reshape.100
  273.4 0.1 copy.52
  273.5 0.1 reshape.101
  273.6 0.1 select_maximum_fusion
  273.7 0.7 reshape.103.refs_4_
  274.3 86.2 %shard_map.311 = (f32[24,2304]{1,0:T(8,128)}, f32[24,768]{1,0:T(8,128)}, f32[96,768]{1,0:T(8,128)}, f32[96,768]{1,0:T(8,128)}, f32[3,128]{1,0:T(4,128)}) custom-call(bf16[2,2,2,4,24,2304]{5,4,3,2,1,0:T(8,128)(2,1)} %bitcast.26, bf16[2,2,2,4,24,768]{5,4,3,2,1,0:T(8,128)(2,1)} %bitcast.27, bf16[2,2,2,4,96,768]{5,4,3,2,1,0:T(8,128)(2,1)} %bitcast.20, ...), custom_call_target="tpu_custom_call" | custom-call | tf_op jit(solution)/shard_map/pallas_call | solution.py:290
  360.5 1.6 fusion
  362.2 1.2 slice.70
  363.4 1.6 fusion.1
  365.0 1.5 copy.62
  366.5 1.7 copy.63
  368.2 1.7 copy.64
  (7 shorter events, 0.1 us)
Async XLA Ops:
  11.2 3.0 copy-start.2
  99.1 6.4 %copy-start.3 = (f32[12,768]{1,0:T(8,128)}, f32[12,768]{1,0:T(8,128)S(1)}, u32[]{:S(2)}) copy-start(f32[12,768]{1,0:T(8,128)S(1)} %constant_dynamic-update-slice_fusion.v_ref) | copy-start | bytes 110596
  244.9 23.5 %copy-start = (bf16[2,529,768]{2,1,0:T(8,128)(2,1)S(1)}, bf16[2,529,768]{2,1,0:T(8,128)(2,1)}, u32[]{:S(2)}) copy-start(bf16[2,529,768]{2,1,0:T(8,128)(2,1)} %get-tuple-element.80) | copy-start | bytes 4875268
  268.3 2.4 copy-start.4
  268.3 2.4 copy-start.5
  268.3 2.4 copy-start.1
